TPU v7x, 32 devices: a whole 2x2x4 slice. The times are simulated.
32 devices in a mesh: section: 4 (over y, x), row: 2 (over core), col: 4 (over z).
Axes of the slice: x: 2, y: 2, z: 4, core: 2. Of those that a mesh axis runs over, the one named last changes fastest.
Arguments:
- cotangent: float32 [4, 128, 4096], P('section', None, ('row', 'col')), may hold values from -6 to 6
- incoming: float32 [4, 128, 4096], P('section', None, ('row', 'col')), may hold values from -6 to 6
- upd_u: float32 [4, 8, 128, 4096], P('section', None, None, ('row', 'col')), may hold values from -4 to 4
- upd_v: float32 [4, 8, 128, 4096], P('section', None, None, ('row', 'col')), may hold values from -0.0078125 to 0.0078125
- saved_x: bfloat16 [4, 4, 128, 4096], P('section', None, None, ('row', 'col')), may hold values from -6 to 6
- saved_h: bfloat16 [4, 4, 2, 128, 14336], P('section', None, None, None, 'col'), may hold values from -6 to 6
- norm_gain: float32 [4, 4096], P('section', ('row', 'col')), may hold values from 0.25 to 1.75
- w_gate: bfloat16 [4, 4096, 14336], P('section', 'row', 'col'), may hold values from -0.09375 to 0.09375
- w_up: bfloat16 [4, 4096, 14336], P('section', 'row', 'col'), may hold values from -0.09375 to 0.09375
- w_down: bfloat16 [4, 14336, 4096], P('section', 'col', 'row'), may hold values from -0.046875 to 0.046875
Outputs:
- new_cotangent: float32 [4, 128, 4096], P('section', None, ('row', 'col'))
- residual_out: float32 [4, 128, 4096], P('section', None, ('row', 'col'))
All inputs are finite; a program needn't handle non-finite values.
Results may differ from a plain program's by a relative error of at most 0.014.
Values may be sent and summed in bfloat16 or wider, within the bound.
No kernel may reach another device: no remote copies, remote signals or barrier semaphores. Data moves between devices by JAX's collectives and lax.ppermute only.
A program may use at most 128 MiB of HBM per device.

v0:
```python
import jax
import jax.numpy as jnp
from jax import lax
from jax.sharding import PartitionSpec as P

D = 4096
eps = 1e-05


def shifted(x, axis, by):
    devices = lax.axis_size(axis)
    return lax.ppermute(x, axis, [(i, (i + by) % devices) for i in range(devices)])


def rotate(carry):
    return shifted(carry, "section", -1)


def shards(cotangent, incoming, upd_u, upd_v, saved_x, saved_h, norm_gain, w_gate, w_up, w_down):
    sections = lax.axis_size("section")
    section_idx = lax.axis_index("section")
    inputs_all = saved_x[0].astype(jnp.float32)
    hidden_all = saved_h[0]
    gain = norm_gain[0]
    wg = w_gate[0]
    wu = w_up[0]
    wd = w_down[0]

    def layer_step(step, carry):
        carry = rotate(carry)
        micro = (section_idx + step + 1) % sections
        xf = lax.dynamic_index_in_dim(inputs_all, micro, 0, keepdims=False)
        hpair = lax.dynamic_index_in_dim(hidden_all, micro, 0, keepdims=False)
        sumsq = lax.psum(jnp.sum(xf * xf, axis=1), ("row", "col"))
        gy = carry.astype(jnp.bfloat16)
        wide = lax.all_gather(gy, "col", axis=1, tiled=True)
        ga_part = lax.dot_general(
            wide, wd, (((1,), (1,)), ((), ())), preferred_element_type=jnp.float32
        )
        ga = lax.psum_scatter(ga_part, "row", scatter_dimension=1, tiled=True)
        width = ga.shape[1]
        offset = lax.axis_index("row") * width
        hg = lax.dynamic_slice_in_dim(hpair[0], offset, width, 1).astype(jnp.float32)
        hu = lax.dynamic_slice_in_dim(hpair[1], offset, width, 1).astype(jnp.float32)
        sig = jax.nn.sigmoid(hg)
        part_gate = (ga * hu * sig * (1.0 + hg * (1.0 - sig))).astype(jnp.bfloat16)
        part_up = (ga * hg * sig).astype(jnp.bfloat16)
        grad_gate, grad_up = (
            lax.all_gather(part_gate, "row", axis=1, tiled=True),
            lax.all_gather(part_up, "row", axis=1, tiled=True),
        )
        first = lax.dot_general(
            wg, grad_gate, (((1,), (1,)), ((), ())), preferred_element_type=jnp.float32
        )
        second = lax.dot_general(
            wu, grad_up, (((1,), (1,)), ((), ())), preferred_element_type=jnp.float32
        )
        normgrad = lax.psum_scatter(first + second, "col", scatter_dimension=0, tiled=True).T
        rstd = lax.rsqrt(sumsq / D + eps)[:, None]
        scaled = gain * normgrad
        inner = lax.psum(jnp.sum(scaled * xf, axis=1), ("row", "col"))[:, None] / D
        updated = carry + rstd * scaled - xf * (rstd * rstd * rstd) * inner
        active = jnp.logical_and(step >= micro, step - micro < sections)
        return jnp.where(active, updated, carry)

    pulled = lax.fori_loop(0, 2 * sections - 1, layer_step, cotangent[0])
    pulled = rotate(pulled)
    resid = pulled + incoming[0] - cotangent[0]
    local_dots = jnp.einsum("urd,rd->u", upd_v[0], resid, precision=lax.Precision.HIGHEST)
    dots = lax.psum(local_dots, ("row", "col"))
    update = jnp.einsum("u,urd->rd", dots, upd_u[0], precision=lax.Precision.HIGHEST)
    fresh = cotangent[0] + resid - update
    return (fresh[None], resid[None])


def solution(mesh):
    placed = (
        P("section", None, ("row", "col")),
        P("section", None, ("row", "col")),
        P("section", None, None, ("row", "col")),
        P("section", None, None, ("row", "col")),
        P("section", None, None, ("row", "col")),
        P("section", None, None, None, "col"),
        P("section", ("row", "col")),
        P("section", "row", "col"),
        P("section", "row", "col"),
        P("section", "col", "row"),
    )
    return jax.shard_map(
        shards,
        mesh=mesh,
        in_specs=placed,
        out_specs=(P("section", None, ("row", "col")), P("section", None, ("row", "col"))),
        check_vma=False,
    )
```

profile of v0, /device:TPU:0, one launch (start us, length us, event | category | flops | bytes accessed | tf_op | source)
XLA Modules:
  0.0 880.5 jit_solution(12553855589407518897)
XLA Ops:
  10.2 832.8 %while.15 = (s32[]{:T(128)}, f32[128,512]{1,0:T(8,128)}, s32[]{:T(128)}, f32[4,128,512]{2,1,0:T(8,128)S(1)}, f32[1,512]{1,0:T(1,128)}, /*index=5*/bf16[3584,2048...) while((s32[]{:T(128)}, f32[128,512]{1,0:T(8,128)}, ...), condition=%wide.region_7.8_spmd, body=%wide.region_0.7_spmd.sunk | while | flops 5641699840 | bytes 72765032 | solution.py:66
  20.1 15.1 %all_gather.33 = bf16[128,2048]{1,0:T(8,128)(2,1)S(1)} all-gather(bf16[128,512]{1,0:T(8,128)(2,1)S(1)} %convert_element_type.72), channel_id=1, replica_groups=mesh['section'=4,'row'=2,'col'=4] {'col'}, dimensions={1}, use_global_device_ids=true | all-gather | bytes 655360 | tf_op jit(solution)/shard_map/while/body/eval_jaxpr/all_gather | solution.py:36
  35.3 11.4 %fusion.48 = f32[128,3584]{1,0:T(8,128)} fusion(bf16[128,2048]{1,0:T(8,128)(2,1)S(1)} %all_gather.33, bf16[3584,2048]{1,0:T(8,128)(2,1)} %get-tuple-element.365), kind=kOutput, calls=%fused_computation.40.clone.1 | convolution fusion | flops 1879048192 | bytes 17039360 | tf_op jit(solution)/shard_map/while/body/eval_jaxpr/dot_general | solution.py:37
  46.7 12.0 %reduce-scatter.3.cloned.1.call-done = f32[128,1792]{1,0:T(8,128)} async-done(((f32[128,3584]{1,0:T(8,128)}), f32[128,1792]{1,0:T(8,128)}) %reduce-scatter.3.cloned.1.call-update) | async-done | bytes 917520 | tf_op jit(solution)/shard_map/while/body/eval_jaxpr/reduce_scatter | solution.py:40
  75.4 10.9 %fusion.51 = f32[2048,128]{0,1:T(8,128)} fusion(f32[128,2048]{1,0:T(8,128)S(1)} %fusion.50, bf16[128,3584]{1,0:T(8,128)(2,1)S(1)} %all_gather.35, bf16[2048,3584]{1,0:T(8,128)(2,1)} %get-tuple-element.368), kind=kOutput, calls=%fused_computation.1.clone.1 | convolution fusion | flops 1879310336 | bytes 17694720 | tf_op jit(solution)/shard_map/while/body/eval_jaxpr/dot_general | solution.py:55
  86.4 28.7 %reduce-scatter.5.cloned.1.call-done = f32[512,128]{0,1:T(8,128)} async-done(((f32[2048,128]{0,1:T(8,128)}), f32[512,128]{0,1:T(8,128)}) %reduce-scatter.5.cloned.1.call-update) | async-done | bytes 262160 | tf_op jit(solution)/shard_map/while/body/eval_jaxpr/reduce_scatter | solution.py:58
  116.2 13.7 %all-reduce.2 = (f32[128]{0:T(128)S(1)}, f32[128]{0:T(128)S(1)}) all-reduce(f32[128]{0:T(128)S(1)} %get-tuple-element.317, f32[128]{0:T(128)S(1)} %get-tuple-element.318), channel_id=1, replica_groups=mesh['section'=4,'row'=2,'col'=4] {'row','col'}, use_global_device_ids=true, to_apply=%region_6.6 | all-reduce | flops 256 | bytes 2048 | tf_op jit(solution)/shard_map/while/body/eval_jaxpr/psum | solution.py:61
  141.1 16.1 %all_gather.33 = bf16[128,2048]{1,0:T(8,128)(2,1)S(1)} all-gather(bf16[128,512]{1,0:T(8,128)(2,1)S(1)} %convert_element_type.72), channel_id=1, replica_groups=mesh['section'=4,'row'=2,'col'=4] {'col'}, dimensions={1}, use_global_device_ids=true | all-gather | bytes 655360 | tf_op jit(solution)/shard_map/while/body/eval_jaxpr/all_gather | solution.py:36
  157.2 11.3 %fusion.48 = f32[128,3584]{1,0:T(8,128)} fusion(bf16[128,2048]{1,0:T(8,128)(2,1)S(1)} %all_gather.33, bf16[3584,2048]{1,0:T(8,128)(2,1)} %get-tuple-element.365), kind=kOutput, calls=%fused_computation.40.clone.1 | convolution fusion | flops 1879048192 | bytes 17039360 | tf_op jit(solution)/shard_map/while/body/eval_jaxpr/dot_general | solution.py:37
  205.0 28.7 %reduce-scatter.5.cloned.1.call-done = f32[512,128]{0,1:T(8,128)} async-done(((f32[2048,128]{0,1:T(8,128)}), f32[512,128]{0,1:T(8,128)}) %reduce-scatter.5.cloned.1.call-update) | async-done | bytes 262160 | tf_op jit(solution)/shard_map/while/body/eval_jaxpr/reduce_scatter | solution.py:58
  234.8 13.7 %all-reduce.2 = (f32[128]{0:T(128)S(1)}, f32[128]{0:T(128)S(1)}) all-reduce(f32[128]{0:T(128)S(1)} %get-tuple-element.317, f32[128]{0:T(128)S(1)} %get-tuple-element.318), channel_id=1, replica_groups=mesh['section'=4,'row'=2,'col'=4] {'row','col'}, use_global_device_ids=true, to_apply=%region_6.6 | all-reduce | flops 256 | bytes 2048 | tf_op jit(solution)/shard_map/while/body/eval_jaxpr/psum | solution.py:61
  259.7 16.2 %all_gather.33 = bf16[128,2048]{1,0:T(8,128)(2,1)S(1)} all-gather(bf16[128,512]{1,0:T(8,128)(2,1)S(1)} %convert_element_type.72), channel_id=1, replica_groups=mesh['section'=4,'row'=2,'col'=4] {'col'}, dimensions={1}, use_global_device_ids=true | all-gather | bytes 655360 | tf_op jit(solution)/shard_map/while/body/eval_jaxpr/all_gather | solution.py:36
  275.8 11.3 %fusion.48 = f32[128,3584]{1,0:T(8,128)} fusion(bf16[128,2048]{1,0:T(8,128)(2,1)S(1)} %all_gather.33, bf16[3584,2048]{1,0:T(8,128)(2,1)} %get-tuple-element.365), kind=kOutput, calls=%fused_computation.40.clone.1 | convolution fusion | flops 1879048192 | bytes 17039360 | tf_op jit(solution)/shard_map/while/body/eval_jaxpr/dot_general | solution.py:37
  323.5 28.7 %reduce-scatter.5.cloned.1.call-done = f32[512,128]{0,1:T(8,128)} async-done(((f32[2048,128]{0,1:T(8,128)}), f32[512,128]{0,1:T(8,128)}) %reduce-scatter.5.cloned.1.call-update) | async-done | bytes 262160 | tf_op jit(solution)/shard_map/while/body/eval_jaxpr/reduce_scatter | solution.py:58
  353.3 13.7 %all-reduce.2 = (f32[128]{0:T(128)S(1)}, f32[128]{0:T(128)S(1)}) all-reduce(f32[128]{0:T(128)S(1)} %get-tuple-element.317, f32[128]{0:T(128)S(1)} %get-tuple-element.318), channel_id=1, replica_groups=mesh['section'=4,'row'=2,'col'=4] {'row','col'}, use_global_device_ids=true, to_apply=%region_6.6 | all-reduce | flops 256 | bytes 2048 | tf_op jit(solution)/shard_map/while/body/eval_jaxpr/psum | solution.py:61
  378.2 16.2 %all_gather.33 = bf16[128,2048]{1,0:T(8,128)(2,1)S(1)} all-gather(bf16[128,512]{1,0:T(8,128)(2,1)S(1)} %convert_element_type.72), channel_id=1, replica_groups=mesh['section'=4,'row'=2,'col'=4] {'col'}, dimensions={1}, use_global_device_ids=true | all-gather | bytes 655360 | tf_op jit(solution)/shard_map/while/body/eval_jaxpr/all_gather | solution.py:36
  394.4 11.3 %fusion.48 = f32[128,3584]{1,0:T(8,128)} fusion(bf16[128,2048]{1,0:T(8,128)(2,1)S(1)} %all_gather.33, bf16[3584,2048]{1,0:T(8,128)(2,1)} %get-tuple-element.365), kind=kOutput, calls=%fused_computation.40.clone.1 | convolution fusion | flops 1879048192 | bytes 17039360 | tf_op jit(solution)/shard_map/while/body/eval_jaxpr/dot_general | solution.py:37
  442.0 28.7 %reduce-scatter.5.cloned.1.call-done = f32[512,128]{0,1:T(8,128)} async-done(((f32[2048,128]{0,1:T(8,128)}), f32[512,128]{0,1:T(8,128)}) %reduce-scatter.5.cloned.1.call-update) | async-done | bytes 262160 | tf_op jit(solution)/shard_map/while/body/eval_jaxpr/reduce_scatter | solution.py:58
  471.8 13.7 %all-reduce.2 = (f32[128]{0:T(128)S(1)}, f32[128]{0:T(128)S(1)}) all-reduce(f32[128]{0:T(128)S(1)} %get-tuple-element.317, f32[128]{0:T(128)S(1)} %get-tuple-element.318), channel_id=1, replica_groups=mesh['section'=4,'row'=2,'col'=4] {'row','col'}, use_global_device_ids=true, to_apply=%region_6.6 | all-reduce | flops 256 | bytes 2048 | tf_op jit(solution)/shard_map/while/body/eval_jaxpr/psum | solution.py:61
  496.7 16.2 %all_gather.33 = bf16[128,2048]{1,0:T(8,128)(2,1)S(1)} all-gather(bf16[128,512]{1,0:T(8,128)(2,1)S(1)} %convert_element_type.72), channel_id=1, replica_groups=mesh['section'=4,'row'=2,'col'=4] {'col'}, dimensions={1}, use_global_device_ids=true | all-gather | bytes 655360 | tf_op jit(solution)/shard_map/while/body/eval_jaxpr/all_gather | solution.py:36
  512.9 11.3 %fusion.48 = f32[128,3584]{1,0:T(8,128)} fusion(bf16[128,2048]{1,0:T(8,128)(2,1)S(1)} %all_gather.33, bf16[3584,2048]{1,0:T(8,128)(2,1)} %get-tuple-element.365), kind=kOutput, calls=%fused_computation.40.clone.1 | convolution fusion | flops 1879048192 | bytes 17039360 | tf_op jit(solution)/shard_map/while/body/eval_jaxpr/dot_general | solution.py:37
  560.6 28.7 %reduce-scatter.5.cloned.1.call-done = f32[512,128]{0,1:T(8,128)} async-done(((f32[2048,128]{0,1:T(8,128)}), f32[512,128]{0,1:T(8,128)}) %reduce-scatter.5.cloned.1.call-update) | async-done | bytes 262160 | tf_op jit(solution)/shard_map/while/body/eval_jaxpr/reduce_scatter | solution.py:58
  590.4 13.7 %all-reduce.2 = (f32[128]{0:T(128)S(1)}, f32[128]{0:T(128)S(1)}) all-reduce(f32[128]{0:T(128)S(1)} %get-tuple-element.317, f32[128]{0:T(128)S(1)} %get-tuple-element.318), channel_id=1, replica_groups=mesh['section'=4,'row'=2,'col'=4] {'row','col'}, use_global_device_ids=true, to_apply=%region_6.6 | all-reduce | flops 256 | bytes 2048 | tf_op jit(solution)/shard_map/while/body/eval_jaxpr/psum | solution.py:61
  615.3 16.2 %all_gather.33 = bf16[128,2048]{1,0:T(8,128)(2,1)S(1)} all-gather(bf16[128,512]{1,0:T(8,128)(2,1)S(1)} %convert_element_type.72), channel_id=1, replica_groups=mesh['section'=4,'row'=2,'col'=4] {'col'}, dimensions={1}, use_global_device_ids=true | all-gather | bytes 655360 | tf_op jit(solution)/shard_map/while/body/eval_jaxpr/all_gather | solution.py:36
  631.5 11.3 %fusion.48 = f32[128,3584]{1,0:T(8,128)} fusion(bf16[128,2048]{1,0:T(8,128)(2,1)S(1)} %all_gather.33, bf16[3584,2048]{1,0:T(8,128)(2,1)} %get-tuple-element.365), kind=kOutput, calls=%fused_computation.40.clone.1 | convolution fusion | flops 1879048192 | bytes 17039360 | tf_op jit(solution)/shard_map/while/body/eval_jaxpr/dot_general | solution.py:37
  679.1 28.7 %reduce-scatter.5.cloned.1.call-done = f32[512,128]{0,1:T(8,128)} async-done(((f32[2048,128]{0,1:T(8,128)}), f32[512,128]{0,1:T(8,128)}) %reduce-scatter.5.cloned.1.call-update) | async-done | bytes 262160 | tf_op jit(solution)/shard_map/while/body/eval_jaxpr/reduce_scatter | solution.py:58
  708.9 13.7 %all-reduce.2 = (f32[128]{0:T(128)S(1)}, f32[128]{0:T(128)S(1)}) all-reduce(f32[128]{0:T(128)S(1)} %get-tuple-element.317, f32[128]{0:T(128)S(1)} %get-tuple-element.318), channel_id=1, replica_groups=mesh['section'=4,'row'=2,'col'=4] {'row','col'}, use_global_device_ids=true, to_apply=%region_6.6 | all-reduce | flops 256 | bytes 2048 | tf_op jit(solution)/shard_map/while/body/eval_jaxpr/psum | solution.py:61
  733.8 16.2 %all_gather.33 = bf16[128,2048]{1,0:T(8,128)(2,1)S(1)} all-gather(bf16[128,512]{1,0:T(8,128)(2,1)S(1)} %convert_element_type.72), channel_id=1, replica_groups=mesh['section'=4,'row'=2,'col'=4] {'col'}, dimensions={1}, use_global_device_ids=true | all-gather | bytes 655360 | tf_op jit(solution)/shard_map/while/body/eval_jaxpr/all_gather | solution.py:36
  750.0 11.3 %fusion.48 = f32[128,3584]{1,0:T(8,128)} fusion(bf16[128,2048]{1,0:T(8,128)(2,1)S(1)} %all_gather.33, bf16[3584,2048]{1,0:T(8,128)(2,1)} %get-tuple-element.365), kind=kOutput, calls=%fused_computation.40.clone.1 | convolution fusion | flops 1879048192 | bytes 17039360 | tf_op jit(solution)/shard_map/while/body/eval_jaxpr/dot_general | solution.py:37
  797.6 28.7 %reduce-scatter.5.cloned.1.call-done = f32[512,128]{0,1:T(8,128)} async-done(((f32[2048,128]{0,1:T(8,128)}), f32[512,128]{0,1:T(8,128)}) %reduce-scatter.5.cloned.1.call-update) | async-done | bytes 262160 | tf_op jit(solution)/shard_map/while/body/eval_jaxpr/reduce_scatter | solution.py:58
  827.4 13.7 %all-reduce.2 = (f32[128]{0:T(128)S(1)}, f32[128]{0:T(128)S(1)}) all-reduce(f32[128]{0:T(128)S(1)} %get-tuple-element.317, f32[128]{0:T(128)S(1)} %get-tuple-element.318), channel_id=1, replica_groups=mesh['section'=4,'row'=2,'col'=4] {'row','col'}, use_global_device_ids=true, to_apply=%region_6.6 | all-reduce | flops 256 | bytes 2048 | tf_op jit(solution)/shard_map/while/body/eval_jaxpr/psum | solution.py:61
  855.4 14.0 %psum.35 = f32[8]{0:T(128)S(1)} all-reduce(f32[8]{0:T(128)S(1)} %fusion.16), channel_id=1, replica_groups=mesh['section'=4,'row'=2,'col'=4] {'row','col'}, use_global_device_ids=true, to_apply=%region_8.9 | all-reduce | flops 8 | bytes 64 | tf_op jit(solution)/shard_map/psum | solution.py:70
  (136 shorter events, 340.7 us)
Async XLA Ops:
  7.2 862.2 %copy-start = (f32[1,8,128,512]{3,2,1,0:T(8,128)S(1)}, f32[1,8,128,512]{3,2,1,0:T(8,128)}, u32[]{:S(2)}) copy-start(f32[1,8,128,512]{3,2,1,0:T(8,128)} %param.14) | copy-start | bytes 6291460
  10.2 48.5 %reduce-scatter.3.cloned.1.call-start = ((), (), s32[]{:S(2)}) async-start(), calls=%async_computation.2 | async-start | bytes 2752512 | tf_op jit(solution)/shard_map/while/body/eval_jaxpr/reduce_scatter | solution.py:40
  10.2 9.9 %collective-permute-start = (f32[128,512]{1,0:T(8,128)}, f32[128,512]{1,0:T(8,128)S(1)}, u32[]{:S(2)}, u32[]{:S(2)}) collective-permute-start(f32[128,512]{1,0:T(8,128)} %get-tuple-element.343), channel_id=1, source_target_pairs={{0,24},{8,0},{16,8},{24,16},{1,25},{9,1},{17,9},{25,17},{2,26},{10... | collective-permute-start | bytes 786440 | tf_op jit(solution)/shard_map/while/body/eval_jaxpr/ppermute | solution.py:12
  46.6 68.5 %reduce-scatter.5.cloned.1.call-start = ((), (), s32[]{:S(2)}) async-start(), calls=%async_computation.3 | async-start | bytes 1310720 | tf_op jit(solution)/shard_map/while/body/eval_jaxpr/reduce_scatter | solution.py:58
  75.4 39.7 %copy-start.2 = (f32[1,512]{1,0:T(1,128)S(1)}, f32[1,512]{1,0:T(1,128)}, u32[]{:S(2)}) copy-start(f32[1,512]{1,0:T(1,128)} %get-tuple-element.364) | copy-start | bytes 6148 | tf_op jit(solution)/shard_map/while
  131.7 45.6 %reduce-scatter.3.cloned.1.call-start = ((), (), s32[]{:S(2)}) async-start(), calls=%async_computation.2 | async-start | bytes 2752512 | tf_op jit(solution)/shard_map/while/body/eval_jaxpr/reduce_scatter | solution.py:40
  131.7 9.4 %collective-permute-start = (f32[128,512]{1,0:T(8,128)}, f32[128,512]{1,0:T(8,128)S(1)}, u32[]{:S(2)}, u32[]{:S(2)}) collective-permute-start(f32[128,512]{1,0:T(8,128)} %get-tuple-element.343), channel_id=1, source_target_pairs={{0,24},{8,0},{16,8},{24,16},{1,25},{9,1},{17,9},{25,17},{2,26},{10... | collective-permute-start | bytes 786440 | tf_op jit(solution)/shard_map/while/body/eval_jaxpr/ppermute | solution.py:12
  168.6 65.1 %reduce-scatter.5.cloned.1.call-start = ((), (), s32[]{:S(2)}) async-start(), calls=%async_computation.3 | async-start | bytes 1310720 | tf_op jit(solution)/shard_map/while/body/eval_jaxpr/reduce_scatter | solution.py:58
  194.0 39.7 %copy-start.2 = (f32[1,512]{1,0:T(1,128)S(1)}, f32[1,512]{1,0:T(1,128)}, u32[]{:S(2)}) copy-start(f32[1,512]{1,0:T(1,128)} %get-tuple-element.364) | copy-start | bytes 6148 | tf_op jit(solution)/shard_map/while
  250.3 45.6 %reduce-scatter.3.cloned.1.call-start = ((), (), s32[]{:S(2)}) async-start(), calls=%async_computation.2 | async-start | bytes 2752512 | tf_op jit(solution)/shard_map/while/body/eval_jaxpr/reduce_scatter | solution.py:40
  250.3 9.4 %collective-permute-start = (f32[128,512]{1,0:T(8,128)}, f32[128,512]{1,0:T(8,128)S(1)}, u32[]{:S(2)}, u32[]{:S(2)}) collective-permute-start(f32[128,512]{1,0:T(8,128)} %get-tuple-element.343), channel_id=1, source_target_pairs={{0,24},{8,0},{16,8},{24,16},{1,25},{9,1},{17,9},{25,17},{2,26},{10... | collective-permute-start | bytes 786440 | tf_op jit(solution)/shard_map/while/body/eval_jaxpr/ppermute | solution.py:12
  287.2 65.0 %reduce-scatter.5.cloned.1.call-start = ((), (), s32[]{:S(2)}) async-start(), calls=%async_computation.3 | async-start | bytes 1310720 | tf_op jit(solution)/shard_map/while/body/eval_jaxpr/reduce_scatter | solution.py:58
  312.6 39.7 %copy-start.2 = (f32[1,512]{1,0:T(1,128)S(1)}, f32[1,512]{1,0:T(1,128)}, u32[]{:S(2)}) copy-start(f32[1,512]{1,0:T(1,128)} %get-tuple-element.364) | copy-start | bytes 6148 | tf_op jit(solution)/shard_map/while
  368.8 45.5 %reduce-scatter.3.cloned.1.call-start = ((), (), s32[]{:S(2)}) async-start(), calls=%async_computation.2 | async-start | bytes 2752512 | tf_op jit(solution)/shard_map/while/body/eval_jaxpr/reduce_scatter | solution.py:40
  368.8 9.4 %collective-permute-start = (f32[128,512]{1,0:T(8,128)}, f32[128,512]{1,0:T(8,128)S(1)}, u32[]{:S(2)}, u32[]{:S(2)}) collective-permute-start(f32[128,512]{1,0:T(8,128)} %get-tuple-element.343), channel_id=1, source_target_pairs={{0,24},{8,0},{16,8},{24,16},{1,25},{9,1},{17,9},{25,17},{2,26},{10... | collective-permute-start | bytes 786440 | tf_op jit(solution)/shard_map/while/body/eval_jaxpr/ppermute | solution.py:12
  405.8 65.0 %reduce-scatter.5.cloned.1.call-start = ((), (), s32[]{:S(2)}) async-start(), calls=%async_computation.3 | async-start | bytes 1310720 | tf_op jit(solution)/shard_map/while/body/eval_jaxpr/reduce_scatter | solution.py:58
  431.1 39.7 %copy-start.2 = (f32[1,512]{1,0:T(1,128)S(1)}, f32[1,512]{1,0:T(1,128)}, u32[]{:S(2)}) copy-start(f32[1,512]{1,0:T(1,128)} %get-tuple-element.364) | copy-start | bytes 6148 | tf_op jit(solution)/shard_map/while
  487.4 45.5 %reduce-scatter.3.cloned.1.call-start = ((), (), s32[]{:S(2)}) async-start(), calls=%async_computation.2 | async-start | bytes 2752512 | tf_op jit(solution)/shard_map/while/body/eval_jaxpr/reduce_scatter | solution.py:40
  487.4 9.4 %collective-permute-start = (f32[128,512]{1,0:T(8,128)}, f32[128,512]{1,0:T(8,128)S(1)}, u32[]{:S(2)}, u32[]{:S(2)}) collective-permute-start(f32[128,512]{1,0:T(8,128)} %get-tuple-element.343), channel_id=1, source_target_pairs={{0,24},{8,0},{16,8},{24,16},{1,25},{9,1},{17,9},{25,17},{2,26},{10... | collective-permute-start | bytes 786440 | tf_op jit(solution)/shard_map/while/body/eval_jaxpr/ppermute | solution.py:12
  524.3 65.0 %reduce-scatter.5.cloned.1.call-start = ((), (), s32[]{:S(2)}) async-start(), calls=%async_computation.3 | async-start | bytes 1310720 | tf_op jit(solution)/shard_map/while/body/eval_jaxpr/reduce_scatter | solution.py:58
  549.6 39.7 %copy-start.2 = (f32[1,512]{1,0:T(1,128)S(1)}, f32[1,512]{1,0:T(1,128)}, u32[]{:S(2)}) copy-start(f32[1,512]{1,0:T(1,128)} %get-tuple-element.364) | copy-start | bytes 6148 | tf_op jit(solution)/shard_map/while
  605.9 45.5 %reduce-scatter.3.cloned.1.call-start = ((), (), s32[]{:S(2)}) async-start(), calls=%async_computation.2 | async-start | bytes 2752512 | tf_op jit(solution)/shard_map/while/body/eval_jaxpr/reduce_scatter | solution.py:40
  605.9 9.4 %collective-permute-start = (f32[128,512]{1,0:T(8,128)}, f32[128,512]{1,0:T(8,128)S(1)}, u32[]{:S(2)}, u32[]{:S(2)}) collective-permute-start(f32[128,512]{1,0:T(8,128)} %get-tuple-element.343), channel_id=1, source_target_pairs={{0,24},{8,0},{16,8},{24,16},{1,25},{9,1},{17,9},{25,17},{2,26},{10... | collective-permute-start | bytes 786440 | tf_op jit(solution)/shard_map/while/body/eval_jaxpr/ppermute | solution.py:12
  642.8 65.0 %reduce-scatter.5.cloned.1.call-start = ((), (), s32[]{:S(2)}) async-start(), calls=%async_computation.3 | async-start | bytes 1310720 | tf_op jit(solution)/shard_map/while/body/eval_jaxpr/reduce_scatter | solution.py:58
  668.1 39.7 %copy-start.2 = (f32[1,512]{1,0:T(1,128)S(1)}, f32[1,512]{1,0:T(1,128)}, u32[]{:S(2)}) copy-start(f32[1,512]{1,0:T(1,128)} %get-tuple-element.364) | copy-start | bytes 6148 | tf_op jit(solution)/shard_map/while
  724.4 45.5 %reduce-scatter.3.cloned.1.call-start = ((), (), s32[]{:S(2)}) async-start(), calls=%async_computation.2 | async-start | bytes 2752512 | tf_op jit(solution)/shard_map/while/body/eval_jaxpr/reduce_scatter | solution.py:40
  724.4 9.4 %collective-permute-start = (f32[128,512]{1,0:T(8,128)}, f32[128,512]{1,0:T(8,128)S(1)}, u32[]{:S(2)}, u32[]{:S(2)}) collective-permute-start(f32[128,512]{1,0:T(8,128)} %get-tuple-element.343), channel_id=1, source_target_pairs={{0,24},{8,0},{16,8},{24,16},{1,25},{9,1},{17,9},{25,17},{2,26},{10... | collective-permute-start | bytes 786440 | tf_op jit(solution)/shard_map/while/body/eval_jaxpr/ppermute | solution.py:12
  761.3 65.0 %reduce-scatter.5.cloned.1.call-start = ((), (), s32[]{:S(2)}) async-start(), calls=%async_computation.3 | async-start | bytes 1310720 | tf_op jit(solution)/shard_map/while/body/eval_jaxpr/reduce_scatter | solution.py:58
  786.6 39.7 %copy-start.2 = (f32[1,512]{1,0:T(1,128)S(1)}, f32[1,512]{1,0:T(1,128)}, u32[]{:S(2)}) copy-start(f32[1,512]{1,0:T(1,128)} %get-tuple-element.364) | copy-start | bytes 6148 | tf_op jit(solution)/shard_map/while
  842.9 9.4 %collective-permute-start.1 = (f32[128,512]{1,0:T(8,128)}, f32[128,512]{1,0:T(8,128)S(1)}, u32[]{:S(2)}, u32[]{:S(2)}) collective-permute-start(f32[128,512]{1,0:T(8,128)} %get-tuple-element.223), channel_id=1, source_target_pairs={{0,24},{8,0},{16,8},{24,16},{1,25},{9,1},{17,9},{25,17},{2,26},{10... | collective-permute-start | bytes 786440 | tf_op jit(solution)/shard_map/ppermute | solution.py:12
  853.4 20.6 %copy-start.1 = (f32[128,512]{1,0:T(8,128)}, f32[128,512]{1,0:T(8,128)S(1)}, u32[]{:S(2)}) copy-start(f32[128,512]{1,0:T(8,128)S(1)} %fusion.20) | copy-start | bytes 786436
Sparse Core Ops, SparseCore 0:
  46.7 11.8 reduce-scatter.2
  86.5 28.5 reduce-scatter.4
  168.7 8.5 reduce-scatter.2
  205.1 28.5 reduce-scatter.4
  287.3 8.4 reduce-scatter.2
  323.6 28.5 reduce-scatter.4
  405.9 8.4 reduce-scatter.2
  442.2 28.5 reduce-scatter.4
  524.4 8.4 reduce-scatter.2
  560.7 28.5 reduce-scatter.4
  642.9 8.4 reduce-scatter.2
  679.2 28.5 reduce-scatter.4
  761.5 8.4 reduce-scatter.2
  797.7 28.5 reduce-scatter.4
where the time goes:
time: 882 us; the launch traced here: 881 us
  waiting for transfers between devices  319 us (36%)
  blocking collectives  256 us (29%)
  matrix products  228 us (26%)
  other arithmetic  39.4 us (4%)
  starting transfers between devices  21 us (2%)
  between operations  13.7 us (2%)
    reduce_scatter x7, waiting for transfers between devices, layer_step(): lax.psum_scatter(first + second, 'col', scatter_dimension=0, tiled=True)  201 us
    all_gather x7, blocking collectives, layer_step(): wide = lax.all_gather(gy, 'col', axis=1, tiled=True)  112 us
    psum x7, blocking collectives, layer_step(): inner = lax.psum(jnp.sum(scaled * xf, axis=1), ('row', 'col'))[:, None] / D  95.9 us
    dot_general x7, matrix products, layer_step(): lax.dot_general(wide, wd, (((1,), (1,)), ((), ())), preferred_element_typ...  79.4 us
    dot_general x7, matrix products, layer_step(): lax.dot_general(wu, grad_up, (((1,), (1,)), ((), ())), preferred_element_...  76.5 us
    dot_general x7, matrix products, layer_step(): lax.dot_general(wg, grad_gate, (((1,), (1,)), ((), ())), preferred_elemen...  69.4 us
    reduce_scatter x7, waiting for transfers between devices, layer_step(): ga = lax.psum_scatter(ga_part, 'row', scatter_dimension=1, tiled=True)  63.1 us
    ppermute x8, waiting for transfers between devices, shifted(): lax.ppermute(x, axis, [(i, (i + by) % devices) for i in range(devices)])  54.8 us
  transfers between devices with their start and end apart: 22, of which 22 were waited for; matrix products, arithmetic and copies ran while one was open for 0% of the time, Pallas kernels for 0%

commit v1 on v0

--- a/solution.py
+++ b/solution.py
@@ -1,3 +1,4 @@
+import functools
 import jax
 import jax.numpy as jnp
 from jax import lax
@@ -5,6 +6,21 @@
 
 D = 4096
 eps = 1e-05
+
+
+def yards_raise(work_x, row_axis):
+    workers = lax.axis_size(row_axis)
+    kept_rows = tuple(((it, (it + 1) % workers) for it in range(workers)))
+    tile_out = [None] * workers
+    tile_out[workers - 1] = work_x
+    for at in range(workers - 2, -1, -1):
+        tile_out[at] = lax.ppermute(tile_out[at + 1], perm=kept_rows, axis_name=row_axis)
+    vec_out = jnp.concatenate(tile_out, axis=1)
+    tmp = (lax.axis_index(row_axis) + 1) * work_x.shape[1]
+    return jnp.roll(vec_out, tmp, axis=1)
+
+
+read_the_axis_part = functools.partial(yards_raise, row_axis="col")
 
 
 def shifted(x, axis, by):
@@ -33,7 +49,7 @@
         hpair = lax.dynamic_index_in_dim(hidden_all, micro, 0, keepdims=False)
         sumsq = lax.psum(jnp.sum(xf * xf, axis=1), ("row", "col"))
         gy = carry.astype(jnp.bfloat16)
-        wide = lax.all_gather(gy, "col", axis=1, tiled=True)
+        wide = read_the_axis_part(gy)
         ga_part = lax.dot_general(
             wide, wd, (((1,), (1,)), ((), ())), preferred_element_type=jnp.float32
         )

time: 882 us -> 915 us (1.037)
  waiting for transfers between devices: 319 us -> 459 us
  blocking collectives: 256 us -> 144 us
    ppermute x0 -> x21, waiting for transfers between devices: none -> 144 us  [yards_raise(): lax.ppermute(tile_out[at + 1], perm=kept_rows, axis_name=row_axis)]
    all_gather x7 -> x0, blocking collectives: 112 us -> none  [layer_step(): wide = lax.all_gather(gy, 'col', axis=1, tiled=True)]
  transfers between devices with their start and end apart: 22 -> 43, of which waited for: 22 -> 43; matrix products, arithmetic and copies ran while one was open for 0% -> 0% of each run, Pallas kernels for 0% -> 0%
where the time goes in v1:
time: 915 us; the launch traced here: 913 us
  waiting for transfers between devices  459 us (50%)
  matrix products  229 us (25%)
  blocking collectives  144 us (16%)
  other arithmetic  40.9 us (4%)
  starting transfers between devices  22.9 us (3%)
  between operations  13.7 us (1%)
    reduce_scatter x7, waiting for transfers between devices, layer_step(): lax.psum_scatter(first + second, 'col', scatter_dimension=0, tiled=True)  201 us
    ppermute x21, waiting for transfers between devices, yards_raise(): lax.ppermute(tile_out[at + 1], perm=kept_rows, axis_name=row_axis)  144 us
    psum x7, blocking collectives, layer_step(): inner = lax.psum(jnp.sum(scaled * xf, axis=1), ('row', 'col'))[:, None] / D  95.9 us
    dot_general x7, matrix products, layer_step(): lax.dot_general(wide, wd, (((1,), (1,)), ((), ())), preferred_element_typ...  79.8 us
    dot_general x7, matrix products, layer_step(): lax.dot_general(wu, grad_up, (((1,), (1,)), ((), ())), preferred_element_...  77.1 us
    dot_general x7, matrix products, layer_step(): lax.dot_general(wg, grad_gate, (((1,), (1,)), ((), ())), preferred_elemen...  69.4 us
    reduce_scatter x7, waiting for transfers between devices, layer_step(): ga = lax.psum_scatter(ga_part, 'row', scatter_dimension=1, tiled=True)  58.8 us
    ppermute x8, waiting for transfers between devices, shifted(): lax.ppermute(x, axis, [(i, (i + by) % devices) for i in range(devices)])  54.8 us
  transfers between devices with their start and end apart: 43, of which 43 were waited for; matrix products, arithmetic and copies ran while one was open for 0% of the time, Pallas kernels for 0%

profile of v1, /device:TPU:0, one launch (start us, length us, event | category | flops | bytes accessed | tf_op | source)
XLA Modules:
  0.0 913.0 jit_solution(5801019085201198227)
XLA Ops:
  11.2 864.3 %while.16 = (s32[]{:T(128)}, f32[128,512]{1,0:T(8,128)}, s32[]{:T(128)}, f32[4,128,512]{2,1,0:T(8,128)}, f32[1,512]{1,0:T(1,128)}, /*index=5*/bf16[3584,2048]{1,...) while((s32[]{:T(128)}, f32[128,512]{1,0:T(8,128)}, ...), condition=%wide.region_7.8_spmd, body=%wide.region_0.7_spmd.sunk | while | flops 5641830912 | bytes 80236528 | solution.py:82
  41.5 11.4 %fusion.49 = f32[128,3584]{1,0:T(8,128)} fusion(bf16[3584,2048]{1,0:T(8,128)(2,1)} %get-tuple-element.407, bf16[128,4096]{1,0:T(8,128)(2,1)S(1)} %constant_dynamic-update-slice_fusion.23, s32[]{:T(128)S(6)} %select_n.117), kind=kOutput, calls=%fused_computation.15.clone.1 | convolution fusion | flops 1879048192 | bytes 17039364 | tf_op jit(solution)/shard_map/while/body/eval_jaxpr/dot_general | solution.py:53
  78.2 11.0 %fusion.52 = f32[2048,128]{0,1:T(8,128)} fusion(f32[128,2048]{1,0:T(8,128)S(1)} %fusion.51, bf16[128,3584]{1,0:T(8,128)(2,1)S(1)} %all_gather.25, bf16[2048,3584]{1,0:T(8,128)(2,1)} %get-tuple-element.410), kind=kOutput, calls=%fused_computation.1.clone.1 | convolution fusion | flops 1879310336 | bytes 17694720 | tf_op jit(solution)/shard_map/while/body/eval_jaxpr/dot_general | solution.py:71
  89.2 28.7 %reduce-scatter.5.cloned.1.call-done = f32[512,128]{0,1:T(8,128)} async-done(((f32[2048,128]{0,1:T(8,128)}), f32[512,128]{0,1:T(8,128)}) %reduce-scatter.5.cloned.1.call-update) | async-done | bytes 262160 | tf_op jit(solution)/shard_map/while/body/eval_jaxpr/reduce_scatter | solution.py:74
  119.0 13.7 %all-reduce.2 = (f32[128]{0:T(128)S(1)}, f32[128]{0:T(128)S(1)}) all-reduce(f32[128]{0:T(128)S(1)} %get-tuple-element.349, f32[128]{0:T(128)S(1)} %get-tuple-element.350), channel_id=1, replica_groups=mesh['section'=4,'row'=2,'col'=4] {'row','col'}, use_global_device_ids=true, to_apply=%region_6.6 | all-reduce | flops 256 | bytes 2048 | tf_op jit(solution)/shard_map/while/body/eval_jaxpr/psum | solution.py:77
  165.0 11.4 %fusion.49 = f32[128,3584]{1,0:T(8,128)} fusion(bf16[3584,2048]{1,0:T(8,128)(2,1)} %get-tuple-element.407, bf16[128,4096]{1,0:T(8,128)(2,1)S(1)} %constant_dynamic-update-slice_fusion.23, s32[]{:T(128)S(6)} %select_n.117), kind=kOutput, calls=%fused_computation.15.clone.1 | convolution fusion | flops 1879048192 | bytes 17039364 | tf_op jit(solution)/shard_map/while/body/eval_jaxpr/dot_general | solution.py:53
  201.7 11.0 %fusion.52 = f32[2048,128]{0,1:T(8,128)} fusion(f32[128,2048]{1,0:T(8,128)S(1)} %fusion.51, bf16[128,3584]{1,0:T(8,128)(2,1)S(1)} %all_gather.25, bf16[2048,3584]{1,0:T(8,128)(2,1)} %get-tuple-element.410), kind=kOutput, calls=%fused_computation.1.clone.1 | convolution fusion | flops 1879310336 | bytes 17694720 | tf_op jit(solution)/shard_map/while/body/eval_jaxpr/dot_general | solution.py:71
  212.7 28.7 %reduce-scatter.5.cloned.1.call-done = f32[512,128]{0,1:T(8,128)} async-done(((f32[2048,128]{0,1:T(8,128)}), f32[512,128]{0,1:T(8,128)}) %reduce-scatter.5.cloned.1.call-update) | async-done | bytes 262160 | tf_op jit(solution)/shard_map/while/body/eval_jaxpr/reduce_scatter | solution.py:74
  242.5 13.7 %all-reduce.2 = (f32[128]{0:T(128)S(1)}, f32[128]{0:T(128)S(1)}) all-reduce(f32[128]{0:T(128)S(1)} %get-tuple-element.349, f32[128]{0:T(128)S(1)} %get-tuple-element.350), channel_id=1, replica_groups=mesh['section'=4,'row'=2,'col'=4] {'row','col'}, use_global_device_ids=true, to_apply=%region_6.6 | all-reduce | flops 256 | bytes 2048 | tf_op jit(solution)/shard_map/while/body/eval_jaxpr/psum | solution.py:77
  288.5 11.4 %fusion.49 = f32[128,3584]{1,0:T(8,128)} fusion(bf16[3584,2048]{1,0:T(8,128)(2,1)} %get-tuple-element.407, bf16[128,4096]{1,0:T(8,128)(2,1)S(1)} %constant_dynamic-update-slice_fusion.23, s32[]{:T(128)S(6)} %select_n.117), kind=kOutput, calls=%fused_computation.15.clone.1 | convolution fusion | flops 1879048192 | bytes 17039364 | tf_op jit(solution)/shard_map/while/body/eval_jaxpr/dot_general | solution.py:53
  325.2 11.0 %fusion.52 = f32[2048,128]{0,1:T(8,128)} fusion(f32[128,2048]{1,0:T(8,128)S(1)} %fusion.51, bf16[128,3584]{1,0:T(8,128)(2,1)S(1)} %all_gather.25, bf16[2048,3584]{1,0:T(8,128)(2,1)} %get-tuple-element.410), kind=kOutput, calls=%fused_computation.1.clone.1 | convolution fusion | flops 1879310336 | bytes 17694720 | tf_op jit(solution)/shard_map/while/body/eval_jaxpr/dot_general | solution.py:71
  336.2 28.7 %reduce-scatter.5.cloned.1.call-done = f32[512,128]{0,1:T(8,128)} async-done(((f32[2048,128]{0,1:T(8,128)}), f32[512,128]{0,1:T(8,128)}) %reduce-scatter.5.cloned.1.call-update) | async-done | bytes 262160 | tf_op jit(solution)/shard_map/while/body/eval_jaxpr/reduce_scatter | solution.py:74
  366.0 13.7 %all-reduce.2 = (f32[128]{0:T(128)S(1)}, f32[128]{0:T(128)S(1)}) all-reduce(f32[128]{0:T(128)S(1)} %get-tuple-element.349, f32[128]{0:T(128)S(1)} %get-tuple-element.350), channel_id=1, replica_groups=mesh['section'=4,'row'=2,'col'=4] {'row','col'}, use_global_device_ids=true, to_apply=%region_6.6 | all-reduce | flops 256 | bytes 2048 | tf_op jit(solution)/shard_map/while/body/eval_jaxpr/psum | solution.py:77
  412.0 11.4 %fusion.49 = f32[128,3584]{1,0:T(8,128)} fusion(bf16[3584,2048]{1,0:T(8,128)(2,1)} %get-tuple-element.407, bf16[128,4096]{1,0:T(8,128)(2,1)S(1)} %constant_dynamic-update-slice_fusion.23, s32[]{:T(128)S(6)} %select_n.117), kind=kOutput, calls=%fused_computation.15.clone.1 | convolution fusion | flops 1879048192 | bytes 17039364 | tf_op jit(solution)/shard_map/while/body/eval_jaxpr/dot_general | solution.py:53
  438.7 9.9 %fusion.51 = f32[128,2048]{1,0:T(8,128)S(1)} fusion(bf16[128,3584]{1,0:T(8,128)(2,1)S(1)} %all_gather.24, bf16[2048,3584]{1,0:T(8,128)(2,1)} %get-tuple-element.409), kind=kOutput, calls=%fused_computation.51.clone.1 | convolution fusion | flops 1879048192 | bytes 16646144 | tf_op jit(solution)/shard_map/while/body/eval_jaxpr/dot_general | solution.py:68
  448.7 11.0 %fusion.52 = f32[2048,128]{0,1:T(8,128)} fusion(f32[128,2048]{1,0:T(8,128)S(1)} %fusion.51, bf16[128,3584]{1,0:T(8,128)(2,1)S(1)} %all_gather.25, bf16[2048,3584]{1,0:T(8,128)(2,1)} %get-tuple-element.410), kind=kOutput, calls=%fused_computation.1.clone.1 | convolution fusion | flops 1879310336 | bytes 17694720 | tf_op jit(solution)/shard_map/while/body/eval_jaxpr/dot_general | solution.py:71
  459.7 28.7 %reduce-scatter.5.cloned.1.call-done = f32[512,128]{0,1:T(8,128)} async-done(((f32[2048,128]{0,1:T(8,128)}), f32[512,128]{0,1:T(8,128)}) %reduce-scatter.5.cloned.1.call-update) | async-done | bytes 262160 | tf_op jit(solution)/shard_map/while/body/eval_jaxpr/reduce_scatter | solution.py:74
  489.5 13.7 %all-reduce.2 = (f32[128]{0:T(128)S(1)}, f32[128]{0:T(128)S(1)}) all-reduce(f32[128]{0:T(128)S(1)} %get-tuple-element.349, f32[128]{0:T(128)S(1)} %get-tuple-element.350), channel_id=1, replica_groups=mesh['section'=4,'row'=2,'col'=4] {'row','col'}, use_global_device_ids=true, to_apply=%region_6.6 | all-reduce | flops 256 | bytes 2048 | tf_op jit(solution)/shard_map/while/body/eval_jaxpr/psum | solution.py:77
  535.5 11.4 %fusion.49 = f32[128,3584]{1,0:T(8,128)} fusion(bf16[3584,2048]{1,0:T(8,128)(2,1)} %get-tuple-element.407, bf16[128,4096]{1,0:T(8,128)(2,1)S(1)} %constant_dynamic-update-slice_fusion.23, s32[]{:T(128)S(6)} %select_n.117), kind=kOutput, calls=%fused_computation.15.clone.1 | convolution fusion | flops 1879048192 | bytes 17039364 | tf_op jit(solution)/shard_map/while/body/eval_jaxpr/dot_general | solution.py:53
  562.2 9.9 %fusion.51 = f32[128,2048]{1,0:T(8,128)S(1)} fusion(bf16[128,3584]{1,0:T(8,128)(2,1)S(1)} %all_gather.24, bf16[2048,3584]{1,0:T(8,128)(2,1)} %get-tuple-element.409), kind=kOutput, calls=%fused_computation.51.clone.1 | convolution fusion | flops 1879048192 | bytes 16646144 | tf_op jit(solution)/shard_map/while/body/eval_jaxpr/dot_general | solution.py:68
  572.1 11.0 %fusion.52 = f32[2048,128]{0,1:T(8,128)} fusion(f32[128,2048]{1,0:T(8,128)S(1)} %fusion.51, bf16[128,3584]{1,0:T(8,128)(2,1)S(1)} %all_gather.25, bf16[2048,3584]{1,0:T(8,128)(2,1)} %get-tuple-element.410), kind=kOutput, calls=%fused_computation.1.clone.1 | convolution fusion | flops 1879310336 | bytes 17694720 | tf_op jit(solution)/shard_map/while/body/eval_jaxpr/dot_general | solution.py:71
  583.2 28.7 %reduce-scatter.5.cloned.1.call-done = f32[512,128]{0,1:T(8,128)} async-done(((f32[2048,128]{0,1:T(8,128)}), f32[512,128]{0,1:T(8,128)}) %reduce-scatter.5.cloned.1.call-update) | async-done | bytes 262160 | tf_op jit(solution)/shard_map/while/body/eval_jaxpr/reduce_scatter | solution.py:74
  613.0 13.7 %all-reduce.2 = (f32[128]{0:T(128)S(1)}, f32[128]{0:T(128)S(1)}) all-reduce(f32[128]{0:T(128)S(1)} %get-tuple-element.349, f32[128]{0:T(128)S(1)} %get-tuple-element.350), channel_id=1, replica_groups=mesh['section'=4,'row'=2,'col'=4] {'row','col'}, use_global_device_ids=true, to_apply=%region_6.6 | all-reduce | flops 256 | bytes 2048 | tf_op jit(solution)/shard_map/while/body/eval_jaxpr/psum | solution.py:77
  659.0 11.4 %fusion.49 = f32[128,3584]{1,0:T(8,128)} fusion(bf16[3584,2048]{1,0:T(8,128)(2,1)} %get-tuple-element.407, bf16[128,4096]{1,0:T(8,128)(2,1)S(1)} %constant_dynamic-update-slice_fusion.23, s32[]{:T(128)S(6)} %select_n.117), kind=kOutput, calls=%fused_computation.15.clone.1 | convolution fusion | flops 1879048192 | bytes 17039364 | tf_op jit(solution)/shard_map/while/body/eval_jaxpr/dot_general | solution.py:53
  695.6 11.0 %fusion.52 = f32[2048,128]{0,1:T(8,128)} fusion(f32[128,2048]{1,0:T(8,128)S(1)} %fusion.51, bf16[128,3584]{1,0:T(8,128)(2,1)S(1)} %all_gather.25, bf16[2048,3584]{1,0:T(8,128)(2,1)} %get-tuple-element.410), kind=kOutput, calls=%fused_computation.1.clone.1 | convolution fusion | flops 1879310336 | bytes 17694720 | tf_op jit(solution)/shard_map/while/body/eval_jaxpr/dot_general | solution.py:71
  706.7 28.7 %reduce-scatter.5.cloned.1.call-done = f32[512,128]{0,1:T(8,128)} async-done(((f32[2048,128]{0,1:T(8,128)}), f32[512,128]{0,1:T(8,128)}) %reduce-scatter.5.cloned.1.call-update) | async-done | bytes 262160 | tf_op jit(solution)/shard_map/while/body/eval_jaxpr/reduce_scatter | solution.py:74
  736.4 13.7 %all-reduce.2 = (f32[128]{0:T(128)S(1)}, f32[128]{0:T(128)S(1)}) all-reduce(f32[128]{0:T(128)S(1)} %get-tuple-element.349, f32[128]{0:T(128)S(1)} %get-tuple-element.350), channel_id=1, replica_groups=mesh['section'=4,'row'=2,'col'=4] {'row','col'}, use_global_device_ids=true, to_apply=%region_6.6 | all-reduce | flops 256 | bytes 2048 | tf_op jit(solution)/shard_map/while/body/eval_jaxpr/psum | solution.py:77
  782.5 11.4 %fusion.49 = f32[128,3584]{1,0:T(8,128)} fusion(bf16[3584,2048]{1,0:T(8,128)(2,1)} %get-tuple-element.407, bf16[128,4096]{1,0:T(8,128)(2,1)S(1)} %constant_dynamic-update-slice_fusion.23, s32[]{:T(128)S(6)} %select_n.117), kind=kOutput, calls=%fused_computation.15.clone.1 | convolution fusion | flops 1879048192 | bytes 17039364 | tf_op jit(solution)/shard_map/while/body/eval_jaxpr/dot_general | solution.py:53
  819.1 11.0 %fusion.52 = f32[2048,128]{0,1:T(8,128)} fusion(f32[128,2048]{1,0:T(8,128)S(1)} %fusion.51, bf16[128,3584]{1,0:T(8,128)(2,1)S(1)} %all_gather.25, bf16[2048,3584]{1,0:T(8,128)(2,1)} %get-tuple-element.410), kind=kOutput, calls=%fused_computation.1.clone.1 | convolution fusion | flops 1879310336 | bytes 17694720 | tf_op jit(solution)/shard_map/while/body/eval_jaxpr/dot_general | solution.py:71
  830.2 28.7 %reduce-scatter.5.cloned.1.call-done = f32[512,128]{0,1:T(8,128)} async-done(((f32[2048,128]{0,1:T(8,128)}), f32[512,128]{0,1:T(8,128)}) %reduce-scatter.5.cloned.1.call-update) | async-done | bytes 262160 | tf_op jit(solution)/shard_map/while/body/eval_jaxpr/reduce_scatter | solution.py:74
  859.9 13.7 %all-reduce.2 = (f32[128]{0:T(128)S(1)}, f32[128]{0:T(128)S(1)}) all-reduce(f32[128]{0:T(128)S(1)} %get-tuple-element.349, f32[128]{0:T(128)S(1)} %get-tuple-element.350), channel_id=1, replica_groups=mesh['section'=4,'row'=2,'col'=4] {'row','col'}, use_global_device_ids=true, to_apply=%region_6.6 | all-reduce | flops 256 | bytes 2048 | tf_op jit(solution)/shard_map/while/body/eval_jaxpr/psum | solution.py:77
  887.9 14.0 %psum.37 = f32[8]{0:T(128)S(1)} all-reduce(f32[8]{0:T(128)S(1)} %fusion.19), channel_id=1, replica_groups=mesh['section'=4,'row'=2,'col'=4] {'row','col'}, use_global_device_ids=true, to_apply=%region_8.9 | all-reduce | flops 8 | bytes 64 | tf_op jit(solution)/shard_map/psum | solution.py:86
  (241 shorter events, 410.6 us)
Async XLA Ops:
  11.2 50.3 %reduce-scatter.3.cloned.1.call-start = ((), (), s32[]{:S(2)}) async-start(), calls=%async_computation.2 | async-start | bytes 2752512 | tf_op jit(solution)/shard_map/while/body/eval_jaxpr/reduce_scatter | solution.py:56
  11.2 9.8 %collective-permute-start = (f32[128,512]{1,0:T(8,128)}, f32[128,512]{1,0:T(8,128)S(1)}, u32[]{:S(2)}, u32[]{:S(2)}) collective-permute-start(f32[128,512]{1,0:T(8,128)} %get-tuple-element.380), channel_id=1, source_target_pairs={{0,24},{8,0},{16,8},{24,16},{1,25},{9,1},{17,9},{25,17},{2,26},{10... | collective-permute-start | bytes 786440 | tf_op jit(solution)/shard_map/while/body/eval_jaxpr/ppermute | solution.py:28
  21.0 6.8 collective-permute-start.1
  27.8 6.8 collective-permute-start.2
  34.6 6.8 collective-permute-start.3
  52.9 65.0 %reduce-scatter.5.cloned.1.call-start = ((), (), s32[]{:S(2)}) async-start(), calls=%async_computation.3 | async-start | bytes 1310720 | tf_op jit(solution)/shard_map/while/body/eval_jaxpr/reduce_scatter | solution.py:74
  134.5 50.4 %reduce-scatter.3.cloned.1.call-start = ((), (), s32[]{:S(2)}) async-start(), calls=%async_computation.2 | async-start | bytes 2752512 | tf_op jit(solution)/shard_map/while/body/eval_jaxpr/reduce_scatter | solution.py:56
  134.5 9.4 %collective-permute-start = (f32[128,512]{1,0:T(8,128)}, f32[128,512]{1,0:T(8,128)S(1)}, u32[]{:S(2)}, u32[]{:S(2)}) collective-permute-start(f32[128,512]{1,0:T(8,128)} %get-tuple-element.380), channel_id=1, source_target_pairs={{0,24},{8,0},{16,8},{24,16},{1,25},{9,1},{17,9},{25,17},{2,26},{10... | collective-permute-start | bytes 786440 | tf_op jit(solution)/shard_map/while/body/eval_jaxpr/ppermute | solution.py:28
  143.9 7.4 collective-permute-start.1
  151.3 6.8 collective-permute-start.2
  176.5 65.0 %reduce-scatter.5.cloned.1.call-start = ((), (), s32[]{:S(2)}) async-start(), calls=%async_computation.3 | async-start | bytes 1310720 | tf_op jit(solution)/shard_map/while/body/eval_jaxpr/reduce_scatter | solution.py:74
  258.0 50.4 %reduce-scatter.3.cloned.1.call-start = ((), (), s32[]{:S(2)}) async-start(), calls=%async_computation.2 | async-start | bytes 2752512 | tf_op jit(solution)/shard_map/while/body/eval_jaxpr/reduce_scatter | solution.py:56
  258.0 9.4 %collective-permute-start = (f32[128,512]{1,0:T(8,128)}, f32[128,512]{1,0:T(8,128)S(1)}, u32[]{:S(2)}, u32[]{:S(2)}) collective-permute-start(f32[128,512]{1,0:T(8,128)} %get-tuple-element.380), channel_id=1, source_target_pairs={{0,24},{8,0},{16,8},{24,16},{1,25},{9,1},{17,9},{25,17},{2,26},{10... | collective-permute-start | bytes 786440 | tf_op jit(solution)/shard_map/while/body/eval_jaxpr/ppermute | solution.py:28
  267.4 7.4 collective-permute-start.1
  300.0 65.0 %reduce-scatter.5.cloned.1.call-start = ((), (), s32[]{:S(2)}) async-start(), calls=%async_computation.3 | async-start | bytes 1310720 | tf_op jit(solution)/shard_map/while/body/eval_jaxpr/reduce_scatter | solution.py:74
  381.5 50.4 %reduce-scatter.3.cloned.1.call-start = ((), (), s32[]{:S(2)}) async-start(), calls=%async_computation.2 | async-start | bytes 2752512 | tf_op jit(solution)/shard_map/while/body/eval_jaxpr/reduce_scatter | solution.py:56
  381.5 9.4 %collective-permute-start = (f32[128,512]{1,0:T(8,128)}, f32[128,512]{1,0:T(8,128)S(1)}, u32[]{:S(2)}, u32[]{:S(2)}) collective-permute-start(f32[128,512]{1,0:T(8,128)} %get-tuple-element.380), channel_id=1, source_target_pairs={{0,24},{8,0},{16,8},{24,16},{1,25},{9,1},{17,9},{25,17},{2,26},{10... | collective-permute-start | bytes 786440 | tf_op jit(solution)/shard_map/while/body/eval_jaxpr/ppermute | solution.py:28
  390.9 7.4 collective-permute-start.1
  423.4 65.0 %reduce-scatter.5.cloned.1.call-start = ((), (), s32[]{:S(2)}) async-start(), calls=%async_computation.3 | async-start | bytes 1310720 | tf_op jit(solution)/shard_map/while/body/eval_jaxpr/reduce_scatter | solution.py:74
  505.0 50.4 %reduce-scatter.3.cloned.1.call-start = ((), (), s32[]{:S(2)}) async-start(), calls=%async_computation.2 | async-start | bytes 2752512 | tf_op jit(solution)/shard_map/while/body/eval_jaxpr/reduce_scatter | solution.py:56
  505.0 9.4 %collective-permute-start = (f32[128,512]{1,0:T(8,128)}, f32[128,512]{1,0:T(8,128)S(1)}, u32[]{:S(2)}, u32[]{:S(2)}) collective-permute-start(f32[128,512]{1,0:T(8,128)} %get-tuple-element.380), channel_id=1, source_target_pairs={{0,24},{8,0},{16,8},{24,16},{1,25},{9,1},{17,9},{25,17},{2,26},{10... | collective-permute-start | bytes 786440 | tf_op jit(solution)/shard_map/while/body/eval_jaxpr/ppermute | solution.py:28
  514.4 7.4 collective-permute-start.1
  546.9 65.0 %reduce-scatter.5.cloned.1.call-start = ((), (), s32[]{:S(2)}) async-start(), calls=%async_computation.3 | async-start | bytes 1310720 | tf_op jit(solution)/shard_map/while/body/eval_jaxpr/reduce_scatter | solution.py:74
  628.5 50.4 %reduce-scatter.3.cloned.1.call-start = ((), (), s32[]{:S(2)}) async-start(), calls=%async_computation.2 | async-start | bytes 2752512 | tf_op jit(solution)/shard_map/while/body/eval_jaxpr/reduce_scatter | solution.py:56
  628.5 9.4 %collective-permute-start = (f32[128,512]{1,0:T(8,128)}, f32[128,512]{1,0:T(8,128)S(1)}, u32[]{:S(2)}, u32[]{:S(2)}) collective-permute-start(f32[128,512]{1,0:T(8,128)} %get-tuple-element.380), channel_id=1, source_target_pairs={{0,24},{8,0},{16,8},{24,16},{1,25},{9,1},{17,9},{25,17},{2,26},{10... | collective-permute-start | bytes 786440 | tf_op jit(solution)/shard_map/while/body/eval_jaxpr/ppermute | solution.py:28
  637.9 7.4 collective-permute-start.1
  670.4 65.0 %reduce-scatter.5.cloned.1.call-start = ((), (), s32[]{:S(2)}) async-start(), calls=%async_computation.3 | async-start | bytes 1310720 | tf_op jit(solution)/shard_map/while/body/eval_jaxpr/reduce_scatter | solution.py:74
  752.0 50.4 %reduce-scatter.3.cloned.1.call-start = ((), (), s32[]{:S(2)}) async-start(), calls=%async_computation.2 | async-start | bytes 2752512 | tf_op jit(solution)/shard_map/while/body/eval_jaxpr/reduce_scatter | solution.py:56
  752.0 9.4 %collective-permute-start = (f32[128,512]{1,0:T(8,128)}, f32[128,512]{1,0:T(8,128)S(1)}, u32[]{:S(2)}, u32[]{:S(2)}) collective-permute-start(f32[128,512]{1,0:T(8,128)} %get-tuple-element.380), channel_id=1, source_target_pairs={{0,24},{8,0},{16,8},{24,16},{1,25},{9,1},{17,9},{25,17},{2,26},{10... | collective-permute-start | bytes 786440 | tf_op jit(solution)/shard_map/while/body/eval_jaxpr/ppermute | solution.py:28
  761.4 7.4 collective-permute-start.1
  793.9 65.0 %reduce-scatter.5.cloned.1.call-start = ((), (), s32[]{:S(2)}) async-start(), calls=%async_computation.3 | async-start | bytes 1310720 | tf_op jit(solution)/shard_map/while/body/eval_jaxpr/reduce_scatter | solution.py:74
  875.5 9.4 %collective-permute-start.4 = (f32[128,512]{1,0:T(8,128)}, f32[128,512]{1,0:T(8,128)S(1)}, u32[]{:S(2)}, u32[]{:S(2)}) collective-permute-start(f32[128,512]{1,0:T(8,128)} %get-tuple-element.255), channel_id=1, source_target_pairs={{0,24},{8,0},{16,8},{24,16},{1,25},{9,1},{17,9},{25,17},{2,26},{10... | collective-permute-start | bytes 786440 | tf_op jit(solution)/shard_map/ppermute | solution.py:28
  (27 other events, 1546.5 us)
Sparse Core Ops, SparseCore 0:
  53.1 8.3 reduce-scatter.2
  89.3 28.5 reduce-scatter.4
  176.6 8.3 reduce-scatter.2
  212.8 28.5 reduce-scatter.4
  300.1 8.3 reduce-scatter.2
  336.3 28.5 reduce-scatter.4
  423.6 8.3 reduce-scatter.2
  459.8 28.5 reduce-scatter.4
  547.0 8.3 reduce-scatter.2
  583.3 28.5 reduce-scatter.4
  670.5 8.3 reduce-scatter.2
  706.8 28.5 reduce-scatter.4
  794.0 8.3 reduce-scatter.2
  830.3 28.5 reduce-scatter.4
